TPU v7x, 128 devices: a whole 4x4x4 slice. The times are simulated.
128 devices in a mesh: aux: 4 (over y), tile: 32 (over x, z, core).
Axes of the slice: x: 4, y: 4, z: 4, core: 2. Of those that a mesh axis runs over, the one named last changes fastest.
Arguments:
- integrals: bfloat16 [11904, 8, 2944], P(('aux', 'tile')), may hold values from -0.57421875 to 0.57421875
- coefficients: bfloat16 [2944, 2048], replicated, may hold values from -0.109375 to 0.109375
- owned_tiles: int32 [2, 64], replicated, may hold values from 0 to 63, each once within a row
- pair_list: int32 [2, 64, 4], P(None, 'tile'), may hold values from -1 to 63, as said below
- amplitudes: bfloat16 [2, 64, 4, 128, 128], P(None, 'tile'), may hold values from -0.25 to 0.25
Outputs:
- residual: float32 [2, 64, 128, 128], P(None, 'tile')
Inputs may be any that keep to these rules, and one draw needn't show every extreme that they name: `pair_list`: every live entry of slot s is a slot within 2 of s; the live entries of one slot are distinct; -1 marks an entry dropped by screening.
All inputs are finite; a program needn't handle non-finite values.
Results may differ from a plain program's by a relative error of at most 0.00087.
Values may be sent and summed in bfloat16 or wider, within the bound.
A program may use at most 128 MiB of HBM per device.

v0:
```python
import jax
import jax.numpy as jnp
from jax import lax
from jax.sharding import PartitionSpec as P

NB = 2


def per_device(integrals, coefficients, owned_tiles, pair_list, amplitudes):
    tile_count = lax.axis_size("tile")
    q_rows, occ_all, ao_count = integrals.shape
    virt_count = coefficients.shape[1]
    tile_width = amplitudes.shape[-1]
    virt_tiles = virt_count // tile_width
    per_dev = pair_list.shape[1]
    occ_batch = occ_all // NB
    total_slots = owned_tiles.shape[1]
    first_slot = lax.axis_index("tile") * per_dev
    positions = jnp.arange(3 * per_dev, dtype=jnp.int32)
    results = []
    for occ_group in range(NB):
        int_block = integrals[:, occ_group * occ_batch : (occ_group + 1) * occ_batch, :].reshape(
            q_rows * occ_batch, ao_count
        )
        half_done = jnp.dot(int_block, coefficients, preferred_element_type=jnp.float32).astype(
            jnp.bfloat16
        )
        half_done = half_done.reshape(q_rows, occ_batch * virt_tiles, tile_width)
        ordered = jnp.take(half_done, owned_tiles[occ_group], axis=1)
        zero_pad = jnp.zeros((q_rows, per_dev, tile_width), jnp.bfloat16)
        padded = jnp.concatenate([zero_pad, ordered, zero_pad], axis=1)
        below_part = padded[:, :total_slots].reshape(q_rows, tile_count, per_dev, tile_width)
        middle = ordered.reshape(q_rows, tile_count, per_dev, tile_width)
        above_part = padded[:, 2 * per_dev :].reshape(q_rows, tile_count, per_dev, tile_width)
        bundle = jnp.concatenate([below_part, middle, above_part], axis=2)
        arrived = lax.all_to_all(bundle, "tile", split_axis=1, concat_axis=0, tiled=True)
        extended = arrived.reshape(q_rows * tile_count, 3 * per_dev, tile_width)
        mine = extended[:, per_dev : 2 * per_dev]
        listed = pair_list[occ_group]
        ext_place = listed - (first_slot - per_dev)
        selector = (
            (ext_place[:, :, None] == positions[None, None, :]) & (listed[:, :, None] >= 0)
        ).astype(jnp.float32)
        amp_tiles = amplitudes[occ_group]
        cross_ints = jnp.einsum("qja,qeb->jeab", mine, extended, preferred_element_type=jnp.float32)
        partial_value = jnp.einsum(
            "jke,jeab->jkab", selector, cross_ints, precision=lax.Precision.HIGHEST
        )
        summed = lax.psum(partial_value, "aux")
        residue = jnp.einsum(
            "jkab,jkbc->jac", summed, amp_tiles.astype(jnp.float32), precision=lax.Precision.HIGHEST
        )
        results.append(residue)
    return jnp.stack(results)


def solution(mesh):
    in_specs = (
        P(("aux", "tile"), None, None),
        P(),
        P(),
        P(None, "tile", None),
        P(None, "tile", None, None, None),
    )
    out_specs = P(None, "tile", None, None)
    return jax.shard_map(
        per_device, mesh=mesh, in_specs=in_specs, out_specs=out_specs, check_vma=False
    )
```

profile of v0, /device:TPU:0, one launch (start us, length us, event | category | flops | bytes accessed | tf_op | source)
XLA Modules:
  0.0 286.1 jit_solution(10070424365951236372)
XLA Ops:
  6.5 0.8 compare_and_fusion.1
  7.3 6.6 %fusion.28 = (bf16[93,4,2944]{2,1,0:T(4,128)(2,1)}, bf16[93,4,2944]{2,1,0:T(4,128)(2,1)S(1)}) fusion(bf16[93,8,2944]{2,1,0:T(8,128)(2,1)} %param.7), kind=kLoop, calls=%fused_computation.51 | loop fusion | bytes 8761344 | tf_op jit(solution)/shard_map/slice | solution.py:22
  13.9 4.4 %reshape.75 = bf16[372,2944]{1,0:T(8,128)(2,1)} reshape(bf16[93,4,2944]{2,1,0:T(4,128)(2,1)} %get-tuple-element.12) | data formatting | bytes 4380672 | tf_op jit(solution)/shard_map/reshape | solution.py:22
  18.3 11.2 %convolution_convert_fusion.1 = bf16[372,2048]{1,0:T(8,128)(2,1)} fusion(bf16[372,2944]{1,0:T(8,128)(2,1)} %reshape.75, bf16[2944,2048]{1,0:T(8,128)(2,1)} %param.8), kind=kOutput, calls=%fused_computation.9 | convolution fusion | flops 4486569984 | bytes 15772672 | tf_op jit(solution)/shard_map/dot_general | solution.py:25
  29.5 3.7 %reshape.76 = bf16[93,64,128]{2,1,0:T(8,128)(2,1)} reshape(bf16[372,2048]{1,0:T(8,128)(2,1)} %convolution_convert_fusion.1) | data formatting | bytes 3047424 | tf_op jit(solution)/shard_map/reshape | solution.py:28
  33.2 3.6 %copy.14 = bf16[93,64,128]{2,0,1:T(8,128)(2,1)} copy(bf16[93,64,128]{2,1,0:T(8,128)(2,1)} %reshape.76) | data formatting | bytes 3047424 | tf_op jit(solution)/shard_map/reshape | solution.py:28
  36.8 2.6 reshape.81
  39.4 10.0 %convolution_convert_fusion = bf16[372,2048]{1,0:T(8,128)(2,1)S(1)} fusion(bf16[372,2944]{1,0:T(8,128)(2,1)} %reshape.81, bf16[2944,2048]{1,0:T(8,128)(2,1)} %param.8), kind=kOutput, calls=%fused_computation.8 | convolution fusion | flops 4486569984 | bytes 15772672 | tf_op jit(solution)/shard_map/dot_general | solution.py:25
  49.4 1.8 reshape.82
  51.3 0.0 copy-start
  51.3 2.5 copy.18
  53.8 0.0 copy-done
  53.8 1.9 gather_fusion
  55.7 1.9 gather_fusion.1
  57.6 2.2 broadcast_select_fusion
  59.8 0.4 pad_slice_fusion.3
  60.3 2.5 pad_maximum_fusion
  62.7 8.4 %all-to-all-start = ((bf16[93,32,6,128]{3,0,2,1:T(8,128)(2,1)}), bf16[93,32,6,128]{3,0,2,1:T(8,128)(2,1)}, u32[]{:S(2)}, u32[]{:S(2)}) async-start(bf16[93,32,6,128]{3,0,2,1:T(8,128)(2,1)} %pad_maximum_fusion), calls=%async_computation | async-start | bytes 9437184 | tf_op jit(solution)/shard_map/all_to_all | solution.py:36
  71.1 0.4 pad_slice_fusion.1
  71.5 2.4 pad_maximum_fusion.1
  73.9 0.0 copy-start.2
  73.9 56.1 %all-to-all-done = bf16[93,32,6,128]{3,0,2,1:T(8,128)(2,1)} async-done(((bf16[93,32,6,128]{3,0,2,1:T(8,128)(2,1)}), bf16[93,32,6,128]{3,0,2,1:T(8,128)(2,1)}, u32[]{:S(2)}, u32[]{:S(2)}) %all-to-all-start) | async-done | bytes 4571168 | tf_op jit(solution)/shard_map/all_to_all | solution.py:36
  130.0 7.2 %all-to-all-start.1 = ((bf16[93,32,6,128]{3,0,2,1:T(8,128)(2,1)}), bf16[93,32,6,128]{3,0,2,1:T(8,128)(2,1)}, u32[]{:S(2)}, u32[]{:S(2)}) async-start(bf16[93,32,6,128]{3,0,2,1:T(8,128)(2,1)} %pad_maximum_fusion.1), calls=%async_computation.1 | async-start | bytes 9437184 | tf_op jit(solution)/shard_map/all_to_all | solution.py:36
  137.3 0.0 all-reduce.7.cloned.1.call-start
  137.4 0.0 copy-done.2
  137.4 5.5 %copy.15 = bf16[32,93,1,6,128]{4,1,0,3,2:T(8,128)(2,1)} copy(bf16[32,93,1,6,128]{4,1,3,0,2:T(8,128)(2,1)} %bitcast.10) | data formatting | bytes 9142272 | tf_op jit(solution)/shard_map/all_to_all | solution.py:36
  142.9 7.4 %reshape.109 = bf16[2976,6,128,1]{2,0,1,3:T(8,128)(2,1)} reshape(bf16[32,93,1,6,128]{4,1,0,3,2:T(8,128)(2,1)} %copy.15) | data formatting | bytes 9142272 | tf_op jit(solution)/shard_map/reshape | solution.py:37
  150.3 7.3 %reshape.80 = bf16[2976,6,128]{2,0,1:T(8,128)(2,1)} reshape(bf16[32,93,1,6,128]{4,1,0,3,2:T(8,128)(2,1)} %copy.15) | data formatting | bytes 9142272 | tf_op jit(solution)/shard_map/reshape | solution.py:37
  157.6 38.8 %all-to-all-done.1 = bf16[93,32,6,128]{3,0,2,1:T(8,128)(2,1)} async-done(((bf16[93,32,6,128]{3,0,2,1:T(8,128)(2,1)}), bf16[93,32,6,128]{3,0,2,1:T(8,128)(2,1)}, u32[]{:S(2)}, u32[]{:S(2)}) %all-to-all-start.1) | async-done | bytes 4571168 | tf_op jit(solution)/shard_map/all_to_all | solution.py:36
  196.4 5.5 %copy.19 = bf16[32,93,1,6,128]{4,1,0,3,2:T(8,128)(2,1)} copy(bf16[32,93,1,6,128]{4,1,3,0,2:T(8,128)(2,1)} %bitcast.28) | data formatting | bytes 9142272 | tf_op jit(solution)/shard_map/all_to_all | solution.py:36
  201.9 7.4 %reshape.113 = bf16[2976,6,128,1]{2,0,1,3:T(8,128)(2,1)} reshape(bf16[32,93,1,6,128]{4,1,0,3,2:T(8,128)(2,1)} %copy.19) | data formatting | bytes 9142272 | tf_op jit(solution)/shard_map/reshape | solution.py:37
  209.3 7.4 %reshape.86 = bf16[2976,6,128]{2,0,1:T(8,128)(2,1)} reshape(bf16[32,93,1,6,128]{4,1,0,3,2:T(8,128)(2,1)} %copy.19) | data formatting | bytes 9142272 | tf_op jit(solution)/shard_map/reshape | solution.py:37
  216.6 4.2 %fusion.4 = f32[2,6,128,128]{2,3,0,1:T(8,128)S(1)} fusion(bf16[2976,6,128]{2,0,1:T(8,128)(2,1)} %reshape.80, bf16[2976,6,128,1]{2,0,1,3:T(8,128)(2,1)} %reshape.109), kind=kOutput, calls=%fused_computation.18 | convolution fusion | flops 1170210816 | bytes 6881280 | tf_op jit(solution)/shard_map/qja,qeb->jeab/dot_general | solution.py:45
  220.8 0.4 copy.16
  221.3 4.2 %fusion.7 = f32[2,6,128,128]{2,3,0,1:T(8,128)S(1)} fusion(bf16[2976,6,128]{2,0,1:T(8,128)(2,1)} %reshape.86, bf16[2976,6,128,1]{2,0,1,3:T(8,128)(2,1)} %reshape.113), kind=kOutput, calls=%fused_computation.19 | convolution fusion | flops 1170210816 | bytes 6881280 | tf_op jit(solution)/shard_map/qja,qeb->jeab/dot_general | solution.py:45
  225.5 0.4 copy.20
  225.9 0.0 copy-start.1
  225.9 1.5 fusion.18
  227.3 1.5 fusion.22
  228.8 0.0 all-reduce.7.cloned.1.call-update
  228.8 46.9 %all-reduce.7.cloned.1.call-done = (f32[2,4,128,128]{3,1,2,0:T(4,128)}, f32[2,4,128,128]{3,1,2,0:T(4,128)}) async-done(((f32[2,4,128,128]{3,1,2,0:T(4,128)}, f32[2,4,128,128]{3,1,2,0:T(4,128)}), (f32[2,4,128,128]{3,1,2,0:T(4,128)}, f32[2,4,128,128]{3,1,2,0:T(4,128)})) %all-reduce.7.cloned.1.call-update) | async-done | bytes 1048592 | tf_op jit(solution)/shard_map/psum | solution.py:49
  275.7 0.0 copy-done.1
  275.7 1.4 convolution_bitcast_fusion
  277.1 1.4 convolution_bitcast_fusion.1
  278.6 0.7 pad_maximum_fusion.2
  (4 shorter events, 0.0 us)
Async XLA Ops:
  51.3 2.5 copy-start
  62.7 67.3 %all-to-all-start = ((bf16[93,32,6,128]{3,0,2,1:T(8,128)(2,1)}), bf16[93,32,6,128]{3,0,2,1:T(8,128)(2,1)}, u32[]{:S(2)}, u32[]{:S(2)}) async-start(bf16[93,32,6,128]{3,0,2,1:T(8,128)(2,1)} %pad_maximum_fusion), calls=%async_computation | async-start | bytes 9437184 | tf_op jit(solution)/shard_map/all_to_all | solution.py:36
  73.9 63.4 %copy-start.2 = (s32[2,2,4]{2,1,0:T(2,128)S(1)}, s32[2,2,4]{2,1,0:T(2,128)}, u32[]{:S(2)}) copy-start(s32[2,2,4]{2,1,0:T(2,128)} %param.10) | copy-start | bytes 196
  130.0 66.4 %all-to-all-start.1 = ((bf16[93,32,6,128]{3,0,2,1:T(8,128)(2,1)}), bf16[93,32,6,128]{3,0,2,1:T(8,128)(2,1)}, u32[]{:S(2)}, u32[]{:S(2)}) async-start(bf16[93,32,6,128]{3,0,2,1:T(8,128)(2,1)} %pad_maximum_fusion.1), calls=%async_computation.1 | async-start | bytes 9437184 | tf_op jit(solution)/shard_map/all_to_all | solution.py:36
  137.3 138.4 %all-reduce.7.cloned.1.call-start = ((), (), s32[]{:S(2)}) async-start(), calls=%async_computation.2 | async-start | bytes 2097152 | tf_op jit(solution)/shard_map/psum | solution.py:49
  225.9 49.8 %copy-start.1 = (bf16[2,2,4,128,128]{4,3,2,1,0:T(8,128)(2,1)S(1)}, bf16[2,2,4,128,128]{4,3,2,1,0:T(8,128)(2,1)}, u32[]{:S(2)}) copy-start(bf16[2,2,4,128,128]{4,3,2,1,0:T(8,128)(2,1)} %param.11) | copy-start | bytes 1572868
Sparse Core Ops, SparseCore 0:
  228.9 46.7 all-reduce.6
where the time goes:
time: 287 us; the launch traced here: 286 us
  waiting for transfers between devices  142 us (49%)
  local copies, waits for them, and re-layouts  71.2 us (25%)
  matrix products  35.3 us (12%)
  starting transfers between devices  15.6 us (5%)
  between operations  13.5 us (5%)
  other arithmetic  8.62 us (3%)
    all_to_all x2, waiting for transfers between devices, per_device(): lax.all_to_all(bundle, 'tile', split_axis=1, concat_axis=0, tiled=True)  94.9 us
    psum x1, waiting for transfers between devices, per_device(): summed = lax.psum(partial_value, 'aux')  46.9 us
    reshape x4, local copies, waits for them, and re-layouts, per_device(): extended = arrived.reshape(q_rows * tile_count, 3 * per_dev, tile_width)  29.5 us
    dot_general x2, matrix products, per_device(): jnp.dot(int_block, coefficients, preferred_element_type=jnp.float32)  21.2 us
    all_to_all x2, starting transfers between devices, per_device(): lax.all_to_all(bundle, 'tile', split_axis=1, concat_axis=0, tiled=True)  15.6 us
    reshape x4, local copies, waits for them, and re-layouts, per_device(): half_done = half_done.reshape(q_rows, occ_batch * virt_tiles, tile_width)  11.6 us
    all_to_all x2, local copies, waits for them, and re-layouts, per_device(): lax.all_to_all(bundle, 'tile', split_axis=1, concat_axis=0, tiled=True)  11 us
    dot_general x2, matrix products, per_device(): jnp.einsum('qja,qeb->jeab', mine, extended, preferred_element_type=jnp.fl...  8.4 us
  transfers between devices with their start and end apart: 3, of which 3 were waited for; matrix products, arithmetic and copies ran while one was open for 8% of the time, Pallas kernels for 0%

commit v1 on v0

--- a/solution.py
+++ b/solution.py
@@ -46,7 +46,8 @@
         partial_value = jnp.einsum(
             "jke,jeab->jkab", selector, cross_ints, precision=lax.Precision.HIGHEST
         )
-        summed = lax.psum(partial_value, "aux")
+        parts = lax.all_gather(partial_value, "aux")
+        summed = jnp.sum(parts, axis=0)
         residue = jnp.einsum(
             "jkab,jkbc->jac", summed, amp_tiles.astype(jnp.float32), precision=lax.Precision.HIGHEST
         )

time: 287 us -> 267 us (0.930)
  waiting for transfers between devices: 142 us -> 119 us
  matrix products: 35.3 us -> 31.6 us
  other arithmetic: 8.62 us -> 12.2 us
    psum x1 -> x0, waiting for transfers between devices: 46.9 us -> none  [per_device(): summed = lax.psum(partial_value, 'aux')]
    all_gather x0 -> x2, waiting for transfers between devices: none -> 30.1 us  [per_device(): parts = lax.all_gather(partial_value, 'aux')]
    all_to_all x2, waiting for transfers between devices: 94.9 us -> 88.9 us  [per_device(): lax.all_to_all(bundle, 'tile', split_axis=1, concat_axis=0, tiled=True)]
    reduce_sum x0 -> x2, other arithmetic: none -> 3.57 us  [per_device(): summed = jnp.sum(parts, axis=0)]
  transfers between devices with their start and end apart: 3 -> 4, of which waited for: 3 -> 3; matrix products, arithmetic and copies ran while one was open for 8% -> 22% of each run, Pallas kernels for 0% -> 0%
where the time goes in v1:
time: 267 us; the launch traced here: 265 us
  waiting for transfers between devices  119 us (45%)
  local copies, waits for them, and re-layouts  72.6 us (27%)
  matrix products  31.6 us (12%)
  starting transfers between devices  15.7 us (6%)
  between operations  13.6 us (5%)
  other arithmetic  12.2 us (5%)
    all_to_all x2, waiting for transfers between devices, per_device(): lax.all_to_all(bundle, 'tile', split_axis=1, concat_axis=0, tiled=True)  88.9 us
    all_gather x2, waiting for transfers between devices, per_device(): parts = lax.all_gather(partial_value, 'aux')  30.1 us
    reshape x4, local copies, waits for them, and re-layouts, per_device(): extended = arrived.reshape(q_rows * tile_count, 3 * per_dev, tile_width)  29.3 us
    dot_general x2, matrix products, per_device(): jnp.dot(int_block, coefficients, preferred_element_type=jnp.float32)  21.2 us
    all_to_all x2, starting transfers between devices, per_device(): lax.all_to_all(bundle, 'tile', split_axis=1, concat_axis=0, tiled=True)  15.6 us
    reshape x4, local copies, waits for them, and re-layouts, per_device(): half_done = half_done.reshape(q_rows, occ_batch * virt_tiles, tile_width)  11.6 us
    all_to_all x2, local copies, waits for them, and re-layouts, per_device(): lax.all_to_all(bundle, 'tile', split_axis=1, concat_axis=0, tiled=True)  10.9 us
    dot_general x2, matrix products, per_device(): jnp.einsum('qja,qeb->jeab', mine, extended, preferred_element_type=jnp.fl...  8.39 us
  transfers between devices with their start and end apart: 4, of which 3 were waited for; matrix products, arithmetic and copies ran while one was open for 22% of the time, Pallas kernels for 0%

profile of v1, /device:TPU:0, one launch (start us, length us, event | category | flops | bytes accessed | tf_op | source)
XLA Modules:
  0.0 264.6 jit_solution(15112325244490030799)
XLA Ops:
  6.5 0.8 compare_and_fusion.1
  7.3 6.6 %fusion.26 = (bf16[93,4,2944]{2,1,0:T(4,128)(2,1)}, bf16[93,4,2944]{2,1,0:T(4,128)(2,1)S(1)}) fusion(bf16[93,8,2944]{2,1,0:T(8,128)(2,1)} %param.7), kind=kLoop, calls=%fused_computation.49 | loop fusion | bytes 8761344 | tf_op jit(solution)/shard_map/slice | solution.py:22
  13.9 4.4 %reshape.75 = bf16[372,2944]{1,0:T(8,128)(2,1)} reshape(bf16[93,4,2944]{2,1,0:T(4,128)(2,1)} %get-tuple-element.10) | data formatting | bytes 4380672 | tf_op jit(solution)/shard_map/reshape | solution.py:22
  18.3 11.2 %convolution_convert_fusion.1 = bf16[372,2048]{1,0:T(8,128)(2,1)} fusion(bf16[372,2944]{1,0:T(8,128)(2,1)} %reshape.75, bf16[2944,2048]{1,0:T(8,128)(2,1)} %param.8), kind=kOutput, calls=%fused_computation.9 | convolution fusion | flops 4486569984 | bytes 15772672 | tf_op jit(solution)/shard_map/dot_general | solution.py:25
  29.5 3.7 %reshape.76 = bf16[93,64,128]{2,1,0:T(8,128)(2,1)} reshape(bf16[372,2048]{1,0:T(8,128)(2,1)} %convolution_convert_fusion.1) | data formatting | bytes 3047424 | tf_op jit(solution)/shard_map/reshape | solution.py:28
  33.2 3.5 %copy.14 = bf16[93,64,128]{2,0,1:T(8,128)(2,1)} copy(bf16[93,64,128]{2,1,0:T(8,128)(2,1)} %reshape.76) | data formatting | bytes 3047424 | tf_op jit(solution)/shard_map/reshape | solution.py:28
  36.7 2.6 reshape.81
  39.4 10.0 %convolution_convert_fusion = bf16[372,2048]{1,0:T(8,128)(2,1)S(1)} fusion(bf16[372,2944]{1,0:T(8,128)(2,1)} %reshape.81, bf16[2944,2048]{1,0:T(8,128)(2,1)} %param.8), kind=kOutput, calls=%fused_computation.8 | convolution fusion | flops 4486569984 | bytes 15772672 | tf_op jit(solution)/shard_map/dot_general | solution.py:25
  49.4 1.8 reshape.82
  51.3 0.0 copy-start
  51.3 2.5 copy.20
  53.8 0.0 copy-done
  53.8 1.9 gather_fusion
  55.7 1.9 gather_fusion.1
  57.6 2.2 broadcast_select_fusion
  59.8 0.4 pad_slice_fusion.3
  60.2 2.4 pad_maximum_fusion
  62.7 8.4 %all-to-all-start = ((bf16[93,32,6,128]{3,0,2,1:T(8,128)(2,1)}), bf16[93,32,6,128]{3,0,2,1:T(8,128)(2,1)}, u32[]{:S(2)}, u32[]{:S(2)}) async-start(bf16[93,32,6,128]{3,0,2,1:T(8,128)(2,1)} %pad_maximum_fusion), calls=%async_computation | async-start | bytes 9437184 | tf_op jit(solution)/shard_map/all_to_all | solution.py:36
  71.0 0.4 pad_slice_fusion.1
  71.4 2.5 pad_maximum_fusion.1
  73.9 0.0 copy-start.2
  73.9 56.1 %all-to-all-done = bf16[93,32,6,128]{3,0,2,1:T(8,128)(2,1)} async-done(((bf16[93,32,6,128]{3,0,2,1:T(8,128)(2,1)}), bf16[93,32,6,128]{3,0,2,1:T(8,128)(2,1)}, u32[]{:S(2)}, u32[]{:S(2)}) %all-to-all-start) | async-done | bytes 4571168 | tf_op jit(solution)/shard_map/all_to_all | solution.py:36
  130.0 7.2 %all-to-all-start.1 = ((bf16[93,32,6,128]{3,0,2,1:T(8,128)(2,1)}), bf16[93,32,6,128]{3,0,2,1:T(8,128)(2,1)}, u32[]{:S(2)}, u32[]{:S(2)}) async-start(bf16[93,32,6,128]{3,0,2,1:T(8,128)(2,1)} %pad_maximum_fusion.1), calls=%async_computation.1 | async-start | bytes 9437184 | tf_op jit(solution)/shard_map/all_to_all | solution.py:36
  137.2 0.0 all-gather.5.cloned.1.call-start
  137.3 0.0 copy-done.2
  137.3 5.4 %copy.15 = bf16[32,93,1,6,128]{4,1,0,3,2:T(8,128)(2,1)} copy(bf16[32,93,1,6,128]{4,1,3,0,2:T(8,128)(2,1)} %bitcast.10) | data formatting | bytes 9142272 | tf_op jit(solution)/shard_map/all_to_all | solution.py:36
  142.8 7.3 %reshape.111 = bf16[2976,6,128,1]{2,0,1,3:T(8,128)(2,1)} reshape(bf16[32,93,1,6,128]{4,1,0,3,2:T(8,128)(2,1)} %copy.15) | data formatting | bytes 9142272 | tf_op jit(solution)/shard_map/reshape | solution.py:37
  150.1 7.3 %reshape.80 = bf16[2976,6,128]{2,0,1:T(8,128)(2,1)} reshape(bf16[32,93,1,6,128]{4,1,0,3,2:T(8,128)(2,1)} %copy.15) | data formatting | bytes 9142272 | tf_op jit(solution)/shard_map/reshape | solution.py:37
  157.4 4.2 %fusion.4 = f32[2,6,128,128]{2,3,0,1:T(8,128)S(1)} fusion(bf16[2976,6,128]{2,0,1:T(8,128)(2,1)} %reshape.80, bf16[2976,6,128,1]{2,0,1,3:T(8,128)(2,1)} %reshape.111), kind=kOutput, calls=%fused_computation.18 | convolution fusion | flops 1170210816 | bytes 6881280 | tf_op jit(solution)/shard_map/qja,qeb->jeab/dot_general | solution.py:45
  161.6 0.4 copy.16
  162.0 0.6 fusion.16
  162.6 0.8 copy.17
  163.5 0.0 all-gather.5.cloned.1.call-update
  163.5 0.0 all-gather.7.cloned.1.call-start
  163.6 32.8 %all-to-all-done.1 = bf16[93,32,6,128]{3,0,2,1:T(8,128)(2,1)} async-done(((bf16[93,32,6,128]{3,0,2,1:T(8,128)(2,1)}), bf16[93,32,6,128]{3,0,2,1:T(8,128)(2,1)}, u32[]{:S(2)}, u32[]{:S(2)}) %all-to-all-start.1) | async-done | bytes 4571168 | tf_op jit(solution)/shard_map/all_to_all | solution.py:36
  196.4 5.5 %copy.21 = bf16[32,93,1,6,128]{4,1,0,3,2:T(8,128)(2,1)} copy(bf16[32,93,1,6,128]{4,1,3,0,2:T(8,128)(2,1)} %bitcast.29) | data formatting | bytes 9142272 | tf_op jit(solution)/shard_map/all_to_all | solution.py:36
  201.9 7.3 %reshape.115 = bf16[2976,6,128,1]{2,0,1,3:T(8,128)(2,1)} reshape(bf16[32,93,1,6,128]{4,1,0,3,2:T(8,128)(2,1)} %copy.21) | data formatting | bytes 9142272 | tf_op jit(solution)/shard_map/reshape | solution.py:37
  209.2 7.3 %reshape.86 = bf16[2976,6,128]{2,0,1:T(8,128)(2,1)} reshape(bf16[32,93,1,6,128]{4,1,0,3,2:T(8,128)(2,1)} %copy.21) | data formatting | bytes 9142272 | tf_op jit(solution)/shard_map/reshape | solution.py:37
  216.5 4.2 %fusion.7 = f32[2,6,128,128]{2,3,0,1:T(8,128)S(1)} fusion(bf16[2976,6,128]{2,0,1:T(8,128)(2,1)} %reshape.86, bf16[2976,6,128,1]{2,0,1,3:T(8,128)(2,1)} %reshape.115), kind=kOutput, calls=%fused_computation.19 | convolution fusion | flops 1170210816 | bytes 6881280 | tf_op jit(solution)/shard_map/qja,qeb->jeab/dot_general | solution.py:45
  220.7 0.4 copy.22
  221.1 0.6 fusion.20
  221.8 0.8 copy.23
  222.6 0.0 all-gather.7.cloned.1.call-update
  222.6 0.0 all-gather.5.cloned.1.call-done
  222.6 0.0 copy-start.1
  222.7 1.8 reduce_sum.18
  224.5 30.1 %all-gather.7.cloned.1.call-done = f32[8,4,128,128]{3,2,1,0:T(8,128)} async-done(((f32[2,4,128,128]{3,2,1,0:T(8,128)}), f32[8,4,128,128]{3,2,1,0:T(8,128)}) %all-gather.7.cloned.1.call-update) | async-done | bytes 2097168 | tf_op jit(solution)/shard_map/all_gather | solution.py:49
  254.5 1.8 reduce_sum.19
  256.3 0.0 copy-done.1
  256.3 0.4 convolution_bitcast_fusion.1
  256.7 0.4 convolution_bitcast_fusion
  257.1 0.7 pad_maximum_fusion.2
  (4 shorter events, 0.0 us)
Async XLA Ops:
  51.3 2.5 copy-start
  62.7 67.3 %all-to-all-start = ((bf16[93,32,6,128]{3,0,2,1:T(8,128)(2,1)}), bf16[93,32,6,128]{3,0,2,1:T(8,128)(2,1)}, u32[]{:S(2)}, u32[]{:S(2)}) async-start(bf16[93,32,6,128]{3,0,2,1:T(8,128)(2,1)} %pad_maximum_fusion), calls=%async_computation | async-start | bytes 9437184 | tf_op jit(solution)/shard_map/all_to_all | solution.py:36
  73.9 63.4 %copy-start.2 = (s32[2,2,4]{2,1,0:T(2,128)S(1)}, s32[2,2,4]{2,1,0:T(2,128)}, u32[]{:S(2)}) copy-start(s32[2,2,4]{2,1,0:T(2,128)} %param.10) | copy-start | bytes 196
  130.0 66.4 %all-to-all-start.1 = ((bf16[93,32,6,128]{3,0,2,1:T(8,128)(2,1)}), bf16[93,32,6,128]{3,0,2,1:T(8,128)(2,1)}, u32[]{:S(2)}, u32[]{:S(2)}) async-start(bf16[93,32,6,128]{3,0,2,1:T(8,128)(2,1)} %pad_maximum_fusion.1), calls=%async_computation.1 | async-start | bytes 9437184 | tf_op jit(solution)/shard_map/all_to_all | solution.py:36
  137.2 85.4 %all-gather.5.cloned.1.call-start = ((), (), s32[]{:S(2)}) async-start(), calls=%async_computation.2 | async-start | bytes 2621440 | tf_op jit(solution)/shard_map/all_gather | solution.py:49
  163.5 91.0 %all-gather.7.cloned.1.call-start = ((), (), s32[]{:S(2)}) async-start(), calls=%async_computation.3 | async-start | bytes 2621440 | tf_op jit(solution)/shard_map/all_gather | solution.py:49
  222.6 33.7 %copy-start.1 = (bf16[2,2,4,128,128]{4,3,2,1,0:T(8,128)(2,1)S(1)}, bf16[2,2,4,128,128]{4,3,2,1,0:T(8,128)(2,1)}, u32[]{:S(2)}) copy-start(bf16[2,2,4,128,128]{4,3,2,1,0:T(8,128)(2,1)} %param.11) | copy-start | bytes 1572868
Sparse Core Ops, SparseCore 0:
  163.6 32.3 all-gather.4
  222.7 31.7 all-gather.6
